TPU v7x, 128 devices: a whole 4x4x4 slice. The times are simulated.
128 devices in a mesh: ctx: 16 (over y, z_hi, core), head: 8 (over x, z_lo).
Axes of the slice: x: 4, y: 4, z: 4 (z_hi: 2, z_lo: 2; z = z_hi * 2 + z_lo), core: 2. Of those that a mesh axis runs over, the one named last changes fastest.
Arguments:
- queries: bfloat16 [2048, 12288], P('ctx', 'head'), may hold values from -8 to 8
- latents: bfloat16 [2048, 512], P('ctx'), may hold values from -4 to 4
- rope_key: bfloat16 [2048, 64], P('ctx'), may hold values from -8 to 8
- up_key_weight: bfloat16 [512, 8192], P(None, 'head'), may hold values from -0.5 to 0.5
- up_value_weight: bfloat16 [512, 8192], P(None, 'head'), may hold values from -0.25 to 0.25
- out_grad: bfloat16 [2048, 8192], P('ctx', 'head'), may hold values from -6 to 6
- group_order: int32 [32], replicated, may hold values from 0 to 31, as said below
Outputs:
- query_grad: bfloat16 [2048, 12288], P('ctx', 'head')
- latent_grad: float32 [2048, 512], P('ctx')
- rope_grad: float32 [2048, 64], P('ctx')
- up_key_grad: float32 [512, 8192], P('ctx', 'head')
- up_value_grad: float32 [512, 8192], P('ctx', 'head')
Inputs may be any that keep to these rules, and one draw needn't show every extreme that they name: A permutation of the 32 group numbers; storage slot k (rows k * 64 to k * 64 + 63) holds the sequence positions group_order[k] * 64 on, in order.
All inputs are finite; a program needn't handle non-finite values.
Results may differ from a plain program's by a relative error of at most 0.017.
Values may be sent and summed in bfloat16 or wider, within the bound.
No kernel may reach another device: no remote copies, remote signals or barrier semaphores. Data moves between devices by JAX's collectives and lax.ppermute only.
A program may use at most 64 MiB of HBM per device.

v0:
```python
import jax
import jax.numpy as jnp
from jax import lax
from jax.sharding import PartitionSpec as P

D_LATENT = 512
ROPE = 64
NOPE = 128
VDIM = 128
NEG_FILL = -1e30


def product(pattern, left_side, right_side):
    return jnp.einsum(pattern, left_side, right_side, preferred_element_type=jnp.float32)


def token_positions(group_order, row_ids, group_len):
    slot_ids = row_ids // group_len
    slot_table = jnp.arange(group_order.shape[0], dtype=jnp.int32)
    picked = jnp.sum(
        jnp.where(slot_ids[:, None] == slot_table[None, :], group_order[None, :], 0), axis=1
    )
    return picked * group_len + row_ids % group_len


def per_device(queries, latents, rope_key, up_key_weight, up_value_weight, out_grad, group_order):
    tok_count = queries.shape[0]
    head_count = up_key_weight.shape[1] // NOPE
    group_len = tok_count // 2
    scale_factor = (NOPE + ROPE) ** (-0.5)
    shaped = queries.reshape(tok_count, head_count, NOPE + ROPE)
    query_nope = shaped[:, :, :NOPE]
    query_rope = shaped[:, :, NOPE:]
    up_key = up_key_weight.reshape(D_LATENT, head_count, NOPE)
    up_value = up_value_weight.reshape(D_LATENT, head_count, VDIM)
    grad_out = out_grad.reshape(tok_count, head_count, VDIM)
    query_abs = product("thd,khd->thk", query_nope, up_key).astype(jnp.bfloat16)
    grad_lat = product("thd,khd->thk", grad_out, up_value).astype(jnp.bfloat16)
    own_rows = lax.axis_index("ctx") * tok_count + jnp.arange(tok_count, dtype=jnp.int32)
    query_pos = token_positions(group_order, own_rows, group_len)

    def piece_scores(latent_piece, rope_piece):
        scores = product("thk,nk->thn", query_abs, latent_piece) + product(
            "thr,nr->thn", query_rope, rope_piece
        )
        return scores * scale_factor

    latent_piece = lax.all_gather(latents, "ctx", axis=0, tiled=True)
    rope_piece = lax.all_gather(rope_key, "ctx", axis=0, tiled=True)
    row_count = latent_piece.shape[0]
    key_pos = token_positions(group_order, jnp.arange(row_count, dtype=jnp.int32), group_len)
    visible = key_pos[None, None, :] <= query_pos[:, None, None]
    run_max = jnp.full((tok_count, head_count), NEG_FILL, jnp.float32)
    scores = piece_scores(latent_piece, rope_piece)
    grad_prob = product("thk,nk->thn", grad_lat, latent_piece)
    new_max = jnp.maximum(run_max, jnp.max(jnp.where(visible, scores, NEG_FILL), axis=2))
    weights = jnp.where(visible, jnp.exp(scores - new_max[:, :, None]), 0.0)
    forward_state = (new_max, jnp.sum(weights, axis=2), jnp.sum(weights * grad_prob, axis=2))
    run_max, run_sum, run_dot = forward_state
    log_total = run_max + jnp.log(run_sum)
    row_delta = run_dot / run_sum
    latent_piece = lax.all_gather(latents, "ctx", axis=0, tiled=True)
    rope_piece = lax.all_gather(rope_key, "ctx", axis=0, tiled=True)
    row_count = latent_piece.shape[0]
    key_pos = token_positions(group_order, jnp.arange(row_count, dtype=jnp.int32), group_len)
    visible = key_pos[None, None, :] <= query_pos[:, None, None]
    scores = piece_scores(latent_piece, rope_piece)
    softmax_rows = jnp.where(visible, jnp.exp(scores - log_total[:, :, None]), 0.0)
    grad_prob = product("thk,nk->thn", grad_lat, latent_piece)
    grad_score = softmax_rows * (grad_prob - row_delta[:, :, None]) * scale_factor
    probs_low = softmax_rows.astype(jnp.bfloat16)
    grad_low = grad_score.astype(jnp.bfloat16)
    acc_out = product("thn,nk->thk", probs_low, latent_piece)
    acc_query = product("thn,nk->thk", grad_low, latent_piece)
    acc_rope = product("thn,nr->thr", grad_low, rope_piece)
    latent_part = product("thn,thk->nk", grad_low, query_abs) + product(
        "thn,thk->nk", probs_low, grad_lat
    )
    rope_part = product("thn,thr->nr", grad_low, query_rope)
    all_latent = latent_part
    all_rope = rope_part
    backward_state = (acc_query, acc_rope, acc_out, all_latent, all_rope)
    acc_query, acc_rope, acc_out, all_latent, all_rope = backward_state
    grad_abs = acc_query.astype(jnp.bfloat16)
    grad_nope = product("thk,khd->thd", grad_abs, up_key)
    query_grad = (
        jnp.concatenate([grad_nope, acc_rope], axis=2).astype(jnp.bfloat16).reshape(tok_count, -1)
    )
    out_low = acc_out.astype(jnp.bfloat16)
    weight_key_grad = product("thk,thd->khd", grad_abs, query_nope).reshape(D_LATENT, -1)
    weight_value_grad = product("thk,thd->khd", out_low, grad_out).reshape(D_LATENT, -1)
    up_key_grad, up_value_grad = (
        lax.psum_scatter(
            weight_key_grad.astype(jnp.bfloat16), "ctx", scatter_dimension=0, tiled=True
        ).astype(jnp.float32),
        lax.psum_scatter(
            weight_value_grad.astype(jnp.bfloat16), "ctx", scatter_dimension=0, tiled=True
        ).astype(jnp.float32),
    )
    partial_latent, partial_rope = (
        lax.psum_scatter(
            all_latent.astype(jnp.bfloat16), "ctx", scatter_dimension=0, tiled=True
        ).astype(jnp.float32),
        lax.psum_scatter(
            all_rope.astype(jnp.bfloat16), "ctx", scatter_dimension=0, tiled=True
        ).astype(jnp.float32),
    )
    latent_grad, rope_grad = (
        lax.psum(partial_latent.astype(jnp.bfloat16), "head").astype(jnp.float32),
        lax.psum(partial_rope.astype(jnp.bfloat16), "head").astype(jnp.float32),
    )
    return (query_grad, latent_grad, rope_grad, up_key_grad, up_value_grad)


def solution(mesh):
    placed = (
        P("ctx", "head"),
        P("ctx", None),
        P("ctx", None),
        P(None, "head"),
        P(None, "head"),
        P("ctx", "head"),
        P(),
    )
    return jax.shard_map(
        per_device,
        mesh=mesh,
        in_specs=placed,
        out_specs=(
            P("ctx", "head"),
            P("ctx", None),
            P("ctx", None),
            P("ctx", "head"),
            P("ctx", "head"),
        ),
        check_vma=False,
    )
```

profile of v0, /device:TPU:0, one launch (start us, length us, event | category | flops | bytes accessed | tf_op | source)
XLA Modules:
  0.0 446.0 jit_solution(16935749232204141822)
XLA Ops:
  13.4 26.6 %all_gather.9 = bf16[2048,64]{0,1:T(8,128)(2,1)S(1)} all-gather(bf16[128,64]{0,1:T(8,128)(2,1)} %param.9), channel_id=1, replica_groups=mesh['ctx'=16,'head'=8] {'ctx'}, dimensions={0}, use_global_device_ids=true | all-gather | bytes 278528 | tf_op jit(solution)/shard_map/all_gather | solution.py:63
  43.2 18.1 %all-gather.2.cloned.1.call-done = bf16[2048,512]{1,0:T(8,128)(2,1)} async-done(((bf16[128,512]{1,0:T(8,128)(2,1)}), bf16[2048,512]{1,0:T(8,128)(2,1)}) %all-gather.2.cloned.1.call-update) | async-done | bytes 2097168 | tf_op jit(solution)/shard_map/all_gather | solution.py:62
  61.3 4.3 fusion.10
  65.6 2.2 select_reduce_fusion
  67.9 4.3 fusion
  72.2 3.2 multiply_convert_fusion
  75.5 2.0 copy-done.1
  77.4 2.4 fusion.46
  79.9 4.7 %fusion.2 = bf16[2048,512]{1,0:T(8,128)(2,1)} fusion(f32[2048,512,1]{1,0,2:T(8,128)S(1)} %fusion.46, bf16[128,8,512]{0,2,1:T(8,128)(2,1)S(1)} %copy-done.6, f32[128,8,2048]{2,0,1:T(8,128)S(1)} %get-tuple-element.30, f32[128,8]{0,1:T(8,128)S(1)} %get-tuple-element.27, pred[128,2048]{1,0:T(8,128)(4,1)S(1)} %broadcast_compare_fusion), kind=kOutput, calls=%fused_computation.9 | convolution fusion | flops 2155872256 | bytes 15994880 | tf_op jit(solution)/shard_map/thn,thk->nk/dot_general | solution.py:14
  84.6 3.0 fusion.3
  88.8 7.7 %convolution_convert_fusion.1 = bf16[8,512,128]{1,2,0:T(8,128)(2,1)} fusion(bf16[128,8,128]{0,2,1:T(8,128)(2,1)S(1)} %bitcast.81, bf16[2048,512]{1,0:T(8,128)(2,1)} %all-gather.2.cloned.1.call-done, f32[128,8,2048]{2,0,1:T(8,128)} %copy-done.2, f32[128,8]{0,1:T(8,128)S(1)} %get-tuple-element.27, pred[128,2048]{1,0:T(8,128)(4,1)S(1)} %broadcast_compare_fusion), kind=kOutput, calls=%fused_computation.21 | convolution fusion | flops 2289041408 | bytes 12062720 | tf_op jit(solution)/shard_map/thk,thd->khd/dot_general | solution.py:14
  96.5 2.3 copy.78
  99.1 5.4 %fusion.12 = bf16[128,8,512]{2,0,1:T(8,128)(2,1)S(1)} fusion(bf16[128,8,2048]{2,0,1:T(8,128)(2,1)} %copy-done.1, bf16[2048,512]{1,0:T(8,128)(2,1)} %all-gather.2.cloned.1.call-done), kind=kOutput, calls=%fused_computation.24 | convolution fusion | flops 2148007936 | bytes 7340032 | tf_op jit(solution)/shard_map/thn,nk->thk/dot_general | solution.py:14
  105.9 2.4 copy.76
  109.4 3.6 convolution_convert_fusion.5
  113.1 41.4 %reduce-scatter.7.cloned.1.call-done = bf16[128,512]{1,0:T(8,128)(2,1)} async-done(((bf16[2048,512]{1,0:T(8,128)(2,1)}), bf16[128,512]{1,0:T(8,128)(2,1)}) %reduce-scatter.7.cloned.1.call-update) | async-done | bytes 131088 | tf_op jit(solution)/shard_map/reduce_scatter | solution.py:101
  155.5 67.5 %reduce-scatter.13.cloned.1.call-done = bf16[128,64]{1,0:T(8,128)(2,1)} async-done(((bf16[2048,64]{1,0:T(8,128)(2,1)}), bf16[128,64]{1,0:T(8,128)(2,1)}) %reduce-scatter.13.cloned.1.call-update) | async-done | bytes 16400
  223.8 33.4 %psum.15 = bf16[128,64]{0,1:T(8,128)(2,1)S(1)} all-reduce(bf16[128,64]{0,1:T(8,128)(2,1)S(1)} %copy.88), channel_id=1, replica_groups=mesh['ctx'=16,'head'=8] {'head'}, use_global_device_ids=true, to_apply=%region_8.9 | all-reduce | flops 8192 | bytes 32768 | tf_op jit(solution)/shard_map/psum | solution.py:110
  257.9 34.8 %reduce-scatter.11.cloned.1.call-done = bf16[32,1024]{1,0:T(8,128)(2,1)} async-done(((bf16[512,1024]{1,0:T(8,128)(2,1)}), bf16[32,1024]{1,0:T(8,128)(2,1)}) %reduce-scatter.11.cloned.1.call-update) | async-done | bytes 65552 | tf_op jit(solution)/shard_map/reduce_scatter | solution.py:96
  292.7 1.5 convert_element_type.89
  294.2 68.2 %reduce-scatter.9.cloned.1.call-done = bf16[32,1024]{1,0:T(8,128)(2,1)} async-done(((bf16[512,1024]{1,0:T(8,128)(2,1)}), bf16[32,1024]{1,0:T(8,128)(2,1)}) %reduce-scatter.9.cloned.1.call-update) | async-done | bytes 65552 | tf_op jit(solution)/shard_map/reduce_scatter | solution.py:93
  362.4 1.5 convert_element_type.84
  363.9 73.6 %all-reduce.2.cloned.1.call-done = bf16[128,512]{1,0:T(8,128)(2,1)} async-done(((bf16[128,512]{1,0:T(8,128)(2,1)}), bf16[128,512]{1,0:T(8,128)(2,1)}) %all-reduce.2.cloned.1.call-update) | async-done | bytes 131088 | tf_op jit(solution)/shard_map/psum | solution.py:109
  437.5 1.6 convert_element_type.78
  (50 shorter events, 15.8 us)
Async XLA Ops:
  7.2 34.3 %copy-start = (bf16[512,1024]{1,0:T(8,128)(2,1)S(1)}, bf16[512,1024]{1,0:T(8,128)(2,1)}, u32[]{:S(2)}) copy-start(bf16[512,1024]{1,0:T(8,128)(2,1)} %param.11) | copy-start | bytes 3145732
  7.2 54.1 %all-gather.2.cloned.1.call-start = ((), (), s32[]{:S(2)}) async-start(), calls=%async_computation.4 | async-start | bytes 2228224 | tf_op jit(solution)/shard_map/all_gather | solution.py:62
  7.9 146.6 %reduce-scatter.7.cloned.1.call-start = ((), (), s32[]{:S(2)}) async-start(), calls=%async_computation.5 | async-start | bytes 2228224 | tf_op jit(solution)/shard_map/reduce_scatter | solution.py:101
  39.9 25.7 %copy-start.3 = (bf16[2048,64]{0,1:T(8,128)(2,1)}, bf16[2048,64]{0,1:T(8,128)(2,1)S(1)}, u32[]{:S(2)}) copy-start(bf16[2048,64]{0,1:T(8,128)(2,1)S(1)} %all_gather.9) | copy-start | bytes 786436
  65.6 2.2 copy-start.6
  65.6 2.2 copy-start.8
  67.8 12.0 %copy-start.2 = (f32[128,8,2048]{2,0,1:T(8,128)}, f32[128,8,2048]{2,0,1:T(8,128)S(1)}, u32[]{:S(2)}) copy-start(f32[128,8,2048]{2,0,1:T(8,128)S(1)} %get-tuple-element.30) | copy-start | bytes 25165828
  72.2 5.2 %copy-start.7 = (bf16[128,8,512]{0,2,1:T(8,128)(2,1)S(1)}, bf16[128,8,512]{0,2,1:T(8,128)(2,1)}, u32[]{:S(2)}) copy-start(bf16[128,8,512]{0,2,1:T(8,128)(2,1)} %fusion.18) | copy-start | bytes 3145732
  75.5 2.0 copy-start.1
  84.6 138.4 %reduce-scatter.13.cloned.1.call-start = ((), (), s32[]{:S(2)}) async-start(), calls=%async_computation.9 | async-start | bytes 557056
  88.7 204.0 %reduce-scatter.11.cloned.1.call-start = ((), (), s32[]{:S(2)}) async-start(), calls=%async_computation.8 | async-start | bytes 1114112 | tf_op jit(solution)/shard_map/reduce_scatter | solution.py:96
  98.8 263.6 %reduce-scatter.9.cloned.1.call-start = ((), (), s32[]{:S(2)}) async-start(), calls=%async_computation.7 | async-start | bytes 1114112 | tf_op jit(solution)/shard_map/reduce_scatter | solution.py:93
  105.9 3.6 copy-start.4
  108.2 329.3 %all-reduce.2.cloned.1.call-start = ((), (), s32[]{:S(2)}) async-start(), calls=%async_computation.6 | async-start | bytes 262144 | tf_op jit(solution)/shard_map/psum | solution.py:109
  109.4 45.1 %copy-start.5 = (bf16[128,8,128]{0,2,1:T(8,128)(2,1)S(1)}, bf16[128,8,128]{0,2,1:T(8,128)(2,1)}, u32[]{:S(2)}) copy-start(bf16[128,8,128]{0,2,1:T(8,128)(2,1)} %fusion.22) | copy-start | bytes 786436
Sparse Core Ops, SparseCore 0:
  10.4 50.8 all-gather.1
  84.7 69.7 reduce-scatter.6
  158.3 64.6 reduce-scatter.12
  226.7 65.9 reduce-scatter.10
  296.4 65.9 reduce-scatter.8
  364.7 72.7 all-reduce.1
where the time goes:
time: 447 us; the launch traced here: 446 us
  waiting for transfers between devices  305 us (68%)
  blocking collectives  60 us (13%)
  matrix products  43.2 us (10%)
  between operations  14.3 us (3%)
  local copies, waits for them, and re-layouts  13.3 us (3%)
  other arithmetic  10.3 us (2%)
    psum x1, waiting for transfers between devices, per_device(): lax.psum(partial_latent.astype(jnp.bfloat16), 'head').astype(jnp.float32)  73.6 us
    unnamed x7, waiting for transfers between devices  68.2 us
    reduce_scatter x1, waiting for transfers between devices, per_device(): lax.psum_scatter(weight_key_grad.astype(jnp.bfloat16), 'ctx', scatter_dim...  68.2 us
    dot_general x13, matrix products, product(): jnp.einsum(pattern, left_side, right_side, preferred_element_type=jnp.flo...  43.2 us
    reduce_scatter x1, waiting for transfers between devices, per_device(): lax.psum_scatter(all_latent.astype(jnp.bfloat16), 'ctx', scatter_dimensio...  41.4 us
    reduce_scatter x1, waiting for transfers between devices, per_device(): lax.psum_scatter(weight_value_grad.astype(jnp.bfloat16), 'ctx', scatter_d...  34.8 us
    psum x1, blocking collectives, per_device(): lax.psum(partial_rope.astype(jnp.bfloat16), 'head').astype(jnp.float32)  33.4 us
    all_gather x1, blocking collectives, per_device(): rope_piece = lax.all_gather(rope_key, 'ctx', axis=0, tiled=True)  26.6 us
  transfers between devices with their start and end apart: 6, of which 6 were waited for; matrix products, arithmetic and copies ran while one was open for 9% of the time, Pallas kernels for 0%

commit v1 on v0

--- a/solution.py
+++ b/solution.py
@@ -2,6 +2,7 @@
 import jax.numpy as jnp
 from jax import lax
 from jax.sharding import PartitionSpec as P
+from jax.lax import all_gather
 
 D_LATENT = 512
 ROPE = 64
@@ -59,8 +60,15 @@
     run_max, run_sum, run_dot = forward_state
     log_total = run_max + jnp.log(run_sum)
     row_delta = run_dot / run_sum
-    latent_piece = lax.all_gather(latents, "ctx", axis=0, tiled=True)
-    rope_piece = lax.all_gather(rope_key, "ctx", axis=0, tiled=True)
+
+    def remake_the_tracks(buf, arr, dev_axis):
+        return jnp.split(
+            all_gather(jnp.concatenate([buf, arr], 1), axis=0, tiled=True, axis_name=dev_axis),
+            [buf.shape[1]],
+            1,
+        )
+
+    latent_piece, rope_piece = remake_the_tracks(latents, rope_key, "ctx")
     row_count = latent_piece.shape[0]
     key_pos = token_positions(group_order, jnp.arange(row_count, dtype=jnp.int32), group_len)
     visible = key_pos[None, None, :] <= query_pos[:, None, None]

time: 447 us -> 492 us (1.10)
  waiting for transfers between devices: 305 us -> 341 us
  matrix products: 43.2 us -> 52.7 us
    all_gather x0 -> x1, waiting for transfers between devices: none -> 38.2 us  [remake_the_tracks(): all_gather(jnp.concatenate([buf, arr], 1), axis=0, tiled=True, axis_name=...]
    dot_general x13 -> x16, matrix products: 43.2 us -> 52.7 us  [product(): jnp.einsum(pattern, left_side, right_side, preferred_element_type=jnp.flo...]
    unnamed x7 -> x8, waiting for transfers between devices: 68.2 us -> 68.1 us
  transfers between devices with their start and end apart: 6 -> 7, of which waited for: 6 -> 7; matrix products, arithmetic and copies ran while one was open for 9% -> 12% of each run, Pallas kernels for 0% -> 0%
where the time goes in v1:
time: 492 us; the launch traced here: 491 us
  waiting for transfers between devices  341 us (69%)
  blocking collectives  59.8 us (12%)
  matrix products  52.7 us (11%)
  between operations  14.4 us (3%)
  local copies, waits for them, and re-layouts  12.1 us (2%)
  other arithmetic  10.7 us (2%)
    psum x1, waiting for transfers between devices, per_device(): lax.psum(partial_latent.astype(jnp.bfloat16), 'head').astype(jnp.float32)  73.8 us
    reduce_scatter x1, waiting for transfers between devices, per_device(): lax.psum_scatter(weight_key_grad.astype(jnp.bfloat16), 'ctx', scatter_dim...  68.2 us
    unnamed x8, waiting for transfers between devices  68.1 us
    dot_general x16, matrix products, product(): jnp.einsum(pattern, left_side, right_side, preferred_element_type=jnp.flo...  52.7 us
    reduce_scatter x1, waiting for transfers between devices, per_device(): lax.psum_scatter(all_latent.astype(jnp.bfloat16), 'ctx', scatter_dimensio...  42.2 us
    all_gather x1, waiting for transfers between devices, remake_the_tracks(): all_gather(jnp.concatenate([buf, arr], 1), axis=0, tiled=True, axis_name=...  38.2 us
    reduce_scatter x1, waiting for transfers between devices, per_device(): lax.psum_scatter(weight_value_grad.astype(jnp.bfloat16), 'ctx', scatter_d...  34.8 us
    psum x1, blocking collectives, per_device(): lax.psum(partial_rope.astype(jnp.bfloat16), 'head').astype(jnp.float32)  33.4 us
  transfers between devices with their start and end apart: 7, of which 7 were waited for; matrix products, arithmetic and copies ran while one was open for 12% of the time, Pallas kernels for 0%

profile of v1, /device:TPU:0, one launch (start us, length us, event | category | flops | bytes accessed | tf_op | source)
XLA Modules:
  0.0 491.2 jit_solution(16925139374184329437)
XLA Ops:
  10.5 26.4 %all_gather.11 = bf16[2048,64]{0,1:T(8,128)(2,1)S(1)} all-gather(bf16[128,64]{0,1:T(8,128)(2,1)} %param.9), channel_id=1, replica_groups=mesh['ctx'=16,'head'=8] {'ctx'}, dimensions={0}, use_global_device_ids=true | all-gather | bytes 278528 | tf_op jit(solution)/shard_map/all_gather | solution.py:50
  45.5 15.9 %all-gather.5.cloned.1.call-done = bf16[2048,512]{1,0:T(8,128)(2,1)} async-done(((bf16[128,512]{1,0:T(8,128)(2,1)}), bf16[2048,512]{1,0:T(8,128)(2,1)}) %all-gather.5.cloned.1.call-update) | async-done | bytes 2097168 | tf_op jit(solution)/shard_map/all_gather | solution.py:49
  61.3 4.3 fusion.8
  65.7 2.2 select_reduce_fusion
  67.9 2.0 fusion.4
  69.9 5.0 %multiply_reduce_fusion = f32[128,8]{0,1:T(8,128)S(1)} fusion(f32[128,8,2048]{2,0,1:T(8,128)S(1)} %get-tuple-element.28, bf16[128,8,512]{0,2,1:T(8,128)(2,1)S(1)} %copy-done.3, f32[128,8]{0,1:T(8,128)S(1)} %broadcast_maximum_fusion, pred[128,2048]{1,0:T(8,128)(4,1)S(1)} %broadcast_compare_fusion, bf16[2048,512]{1,0:T(8,128)(2,1)S(1)} %copy-done.7), kind=kOutput, calls=%fused_computation.6 | convolution fusion | flops 2155871232 | bytes 11804672 | tf_op jit(solution)/shard_map/thk,nk->thn/dot_general | solution.py:15
  74.9 38.2 %all-gather.3.cloned.1.call-done = bf16[2048,576]{1,0:T(8,128)(2,1)} async-done(((bf16[128,576]{1,0:T(8,128)(2,1)}), bf16[2048,576]{1,0:T(8,128)(2,1)}) %all-gather.3.cloned.1.call-update) | async-done | bytes 2359312 | tf_op jit(solution)/shard_map/all_gather | solution.py:66
  113.2 4.4 fusion.23
  117.6 2.6 fusion.3
  120.3 3.2 multiply_convert_fusion
  123.5 2.4 fusion.40
  126.0 4.0 fusion.5
  130.0 3.0 fusion.6
  134.1 7.7 %convolution_convert_fusion.1 = bf16[8,512,128]{1,2,0:T(8,128)(2,1)} fusion(bf16[128,8,128]{0,2,1:T(8,128)(2,1)S(1)} %bitcast.92, f32[128,8,2048]{2,0,1:T(8,128)} %copy-done.2, bf16[2048,576]{1,0:T(8,128)(2,1)} %all-gather.3.cloned.1.call-done), kind=kOutput, calls=%fused_computation.23 | convolution fusion | flops 2284847104 | bytes 11796480 | tf_op jit(solution)/shard_map/thk,thd->khd/dot_general | solution.py:15
  141.8 2.3 copy.103
  144.2 5.4 %convolution_convert_fusion.4 = bf16[128,8,512]{2,0,1:T(8,128)(2,1)S(1)} fusion(bf16[128,8,2048]{2,0,1:T(8,128)(2,1)} %copy-done.1, bf16[2048,576]{1,0:T(8,128)(2,1)} %all-gather.3.cloned.1.call-done), kind=kOutput, calls=%fused_computation.27 | convolution fusion | flops 2148007936 | bytes 7340032 | tf_op jit(solution)/shard_map/thn,nk->thk/dot_general | solution.py:15
  151.0 2.3 copy.101
  153.8 3.7 convolution_convert_fusion.6
  157.5 42.2 %reduce-scatter.7.cloned.1.call-done = bf16[128,512]{1,0:T(8,128)(2,1)} async-done(((bf16[2048,512]{1,0:T(8,128)(2,1)}), bf16[128,512]{1,0:T(8,128)(2,1)}) %reduce-scatter.7.cloned.1.call-update) | async-done | bytes 131088 | tf_op jit(solution)/shard_map/reduce_scatter | solution.py:109
  200.7 67.3 %reduce-scatter.13.cloned.1.call-done = bf16[128,64]{1,0:T(8,128)(2,1)} async-done(((bf16[2048,64]{1,0:T(8,128)(2,1)}), bf16[128,64]{1,0:T(8,128)(2,1)}) %reduce-scatter.13.cloned.1.call-update) | async-done | bytes 16400
  268.9 33.4 %psum.15 = bf16[128,64]{0,1:T(8,128)(2,1)S(1)} all-reduce(bf16[128,64]{0,1:T(8,128)(2,1)S(1)} %copy.120), channel_id=1, replica_groups=mesh['ctx'=16,'head'=8] {'head'}, use_global_device_ids=true, to_apply=%region_8.9 | all-reduce | flops 8192 | bytes 32768 | tf_op jit(solution)/shard_map/psum | solution.py:118
  302.9 34.8 %reduce-scatter.11.cloned.1.call-done = bf16[32,1024]{1,0:T(8,128)(2,1)} async-done(((bf16[512,1024]{1,0:T(8,128)(2,1)}), bf16[32,1024]{1,0:T(8,128)(2,1)}) %reduce-scatter.11.cloned.1.call-update) | async-done | bytes 65552 | tf_op jit(solution)/shard_map/reduce_scatter | solution.py:104
  339.2 68.2 %reduce-scatter.9.cloned.1.call-done = bf16[32,1024]{1,0:T(8,128)(2,1)} async-done(((bf16[512,1024]{1,0:T(8,128)(2,1)}), bf16[32,1024]{1,0:T(8,128)(2,1)}) %reduce-scatter.9.cloned.1.call-update) | async-done | bytes 65552 | tf_op jit(solution)/shard_map/reduce_scatter | solution.py:101
  408.9 73.8 %all-reduce.2.cloned.1.call-done = bf16[128,512]{1,0:T(8,128)(2,1)} async-done(((bf16[128,512]{1,0:T(8,128)(2,1)}), bf16[128,512]{1,0:T(8,128)(2,1)}) %all-reduce.2.cloned.1.call-update) | async-done | bytes 131088 | tf_op jit(solution)/shard_map/psum | solution.py:117
  (56 shorter events, 22.0 us)
Async XLA Ops:
  7.2 35.1 %copy-start = (bf16[512,1024]{1,0:T(8,128)(2,1)S(1)}, bf16[512,1024]{1,0:T(8,128)(2,1)}, u32[]{:S(2)}) copy-start(bf16[512,1024]{1,0:T(8,128)(2,1)} %param.11) | copy-start | bytes 3145732
  7.2 54.2 %all-gather.5.cloned.1.call-start = ((), (), s32[]{:S(2)}) async-start(), calls=%async_computation.5 | async-start | bytes 2228224 | tf_op jit(solution)/shard_map/all_gather | solution.py:49
  7.9 105.3 %all-gather.3.cloned.1.call-start = ((), (), s32[]{:S(2)}) async-start(), calls=%async_computation.4 | async-start | bytes 2785280 | tf_op jit(solution)/shard_map/all_gather | solution.py:66
  10.4 189.3 %reduce-scatter.7.cloned.1.call-start = ((), (), s32[]{:S(2)}) async-start(), calls=%async_computation.6 | async-start | bytes 2228224 | tf_op jit(solution)/shard_map/reduce_scatter | solution.py:109
  67.9 2.0 copy-start.3
  67.9 2.0 copy-start.7
  113.2 4.5 copy-start.6
  117.6 2.6 copy-start.4
  120.2 5.7 %copy-start.2 = (f32[128,8,2048]{2,0,1:T(8,128)}, f32[128,8,2048]{2,0,1:T(8,128)S(1)}, u32[]{:S(2)}) copy-start(f32[128,8,2048]{2,0,1:T(8,128)S(1)} %fusion.3) | copy-start | bytes 25165828
  120.2 3.3 copy-start.5
  123.5 2.4 copy-start.1
  130.0 138.1 %reduce-scatter.13.cloned.1.call-start = ((), (), s32[]{:S(2)}) async-start(), calls=%async_computation.10 | async-start | bytes 557056
  134.1 203.6 %reduce-scatter.11.cloned.1.call-start = ((), (), s32[]{:S(2)}) async-start(), calls=%async_computation.9 | async-start | bytes 1114112 | tf_op jit(solution)/shard_map/reduce_scatter | solution.py:104
  144.2 263.2 %reduce-scatter.9.cloned.1.call-start = ((), (), s32[]{:S(2)}) async-start(), calls=%async_computation.8 | async-start | bytes 1114112 | tf_op jit(solution)/shard_map/reduce_scatter | solution.py:101
  153.3 329.4 %all-reduce.2.cloned.1.call-start = ((), (), s32[]{:S(2)}) async-start(), calls=%async_computation.7 | async-start | bytes 262144 | tf_op jit(solution)/shard_map/psum | solution.py:117
Sparse Core Ops, SparseCore 0:
  10.4 50.9 all-gather.4
  64.3 48.8 all-gather.2
  130.1 69.6 reduce-scatter.6
  203.3 64.6 reduce-scatter.12
  271.7 65.9 reduce-scatter.10
  341.4 65.9 reduce-scatter.8
  409.9 72.8 all-reduce.1
